TPU v7x, 32 devices: a whole 2x2x4 slice. The times are simulated.
32 devices in a mesh: ctx: 8 (over z, x), tp: 4 (over y, core).
Axes of the slice: x: 2, y: 2, z: 4, core: 2. Of those that a mesh axis runs over, the one named last changes fastest.
Arguments:
- inputs: bfloat16 [4096, 768], P(('ctx', 'tp')), may hold values from -6 to 6
- positions: int32 [4096], P('ctx'), may hold values from 0 to 3071, as said below
- attn_scale: float32 [768], replicated, may hold values from 0.1 to 1.9
- attn_shift: float32 [768], replicated, may hold values from -4 to 4
- mlp_scale: float32 [768], replicated, may hold values from 0.1 to 1.9
- mlp_shift: float32 [768], replicated, may hold values from -4 to 4
- qkv_weight: bfloat16 [768, 3, 768], P(None, None, 'tp'), may hold values from -0.21875 to 0.21875
- qv_bias: float32 [2, 768], P(None, 'tp'), may hold values from -4 to 4
- dense_weight: bfloat16 [768, 768], P('tp'), may hold values from -1.75 to 1.75
- dense_bias: float32 [768], replicated, may hold values from -5 to 5
- up_weight: bfloat16 [768, 3072], P(None, 'tp'), may hold values from -0.21875 to 0.21875
- up_bias: float32 [3072], P('tp'), may hold values from -4 to 4
- down_weight: bfloat16 [3072, 768], P('tp'), may hold values from -0.109375 to 0.109375
- down_bias: float32 [768], replicated, may hold values from -5 to 5
- cotangent: bfloat16 [4096, 768], P(('ctx', 'tp')), may hold values from -6 to 6
Outputs:
- output: bfloat16 [4096, 768], P(('ctx', 'tp'))
- grad_input: float32 [4096, 768], P(('ctx', 'tp'))
- grad_attn_scale: float32 [768], replicated
- grad_attn_shift: float32 [768], replicated
- grad_mlp_scale: float32 [768], replicated
- grad_mlp_shift: float32 [768], replicated
- grad_qkv: float32 [768, 3, 768], P(None, None, 'tp')
- grad_qv_bias: float32 [2, 768], P(None, 'tp')
- grad_dense: float32 [768, 768], P('tp')
- grad_dense_bias: float32 [768], replicated
- grad_up: float32 [768, 3072], P(None, 'tp')
- grad_up_bias: float32 [3072], P('tp')
- grad_down: float32 [3072, 768], P('tp')
- grad_down_bias: float32 [768], replicated
Inputs may be any that keep to these rules, and one draw needn't show every extreme that they name: The sequence holds three documents; positions count from 0 at each document's first token and rise by one along it; the second document has 3072 tokens and starts at a token between 1 and 1023.
All inputs are finite; a program needn't handle non-finite values.
Results may differ from a plain program's by a relative error of at most 0.025.
Values may be sent and summed in bfloat16 or wider, within the bound.
A program may use at most 128 MiB of HBM per device.

v0:
```python
import math
import jax
import jax.numpy as jnp
from jax import lax
from jax.sharding import PartitionSpec as P

D = 768
HD = 64
ROT = 16
norm_eps = 1e-05


def layer_norm(values, scale, shift):
    mean_value = jnp.mean(values, axis=-1, keepdims=True)
    centred = values - mean_value
    variance = jnp.mean(centred * centred, axis=-1, keepdims=True)
    inv_std = lax.rsqrt(variance + norm_eps)
    normal_part = centred * inv_std
    return (normal_part * scale + shift, normal_part, inv_std)


def norm_backward(grad_normed, normal_part, inv_std, scale):
    grad_hat = grad_normed * scale
    mean_grad = jnp.mean(grad_hat, axis=-1, keepdims=True)
    mean_mixed = jnp.mean(grad_hat * normal_part, axis=-1, keepdims=True)
    return inv_std * (grad_hat - mean_grad - normal_part * mean_mixed)


def rotary_tables(positions):
    freqs = 10000.0 ** (-jnp.arange(0, ROT, 2).astype(jnp.float32) / ROT)
    angles = positions.astype(jnp.float32)[:, None] * freqs[None, :]
    angles = jnp.concatenate([angles, angles], axis=1)
    return (jnp.cos(angles), jnp.sin(angles))


def rotate(tensor, cosines, sines):
    part = tensor[..., :ROT]
    half = ROT // 2
    turned = jnp.concatenate([-part[..., half:], part[..., :half]], axis=-1)
    spun = part * cosines[:, None, :] + turned * sines[:, None, :]
    return jnp.concatenate([spun, tensor[..., ROT:]], axis=-1)


def gelu_grad(pre_act):
    cumulative = 0.5 * (1.0 + jax.scipy.special.erf(pre_act * 0.7071067811865476))
    density = jnp.exp(-0.5 * pre_act * pre_act) * 0.3989422804014327
    return cumulative + pre_act * density


def block_length(length):
    return math.gcd(length, 1024)


def local(
    inputs,
    positions,
    attn_scale,
    attn_shift,
    mlp_scale,
    mlp_shift,
    qkv_weight,
    qv_bias,
    dense_weight,
    dense_bias,
    up_weight,
    up_bias,
    down_weight,
    down_bias,
    cotangent,
):
    local_width = qkv_weight.shape[2]
    head_count = local_width // HD
    score_scale = HD ** (-0.5)
    resid = inputs.astype(jnp.float32)
    normed_one, hat_one, std_one = layer_norm(resid, attn_scale, attn_shift)
    normed_two, hat_two, std_two = layer_norm(resid, mlp_scale, mlp_shift)
    attn_in, mlp_in = (
        lax.all_gather(normed_one.astype(jnp.bfloat16), "tp", axis=0, tiled=True),
        lax.all_gather(normed_two.astype(jnp.bfloat16), "tp", axis=0, tiled=True),
    )
    block_rows = attn_in.shape[0]
    proj = jnp.dot(
        attn_in, qkv_weight.reshape(D, 3 * local_width), preferred_element_type=jnp.float32
    )
    proj = proj.reshape(block_rows, 3, head_count, HD)
    cosines, sines = rotary_tables(positions)
    queries = rotate(proj[:, 0] + qv_bias[0].reshape(head_count, HD), cosines, sines).astype(
        jnp.bfloat16
    )
    keys_rot = rotate(proj[:, 1], cosines, sines).astype(jnp.bfloat16)
    values = (proj[:, 2] + qv_bias[1].reshape(head_count, HD)).astype(jnp.bfloat16)
    own_start = lax.axis_index("ctx") * block_rows
    query_pos = own_start + jnp.arange(block_rows, dtype=jnp.int32)
    first_key = query_pos - positions
    last_query = query_pos[block_rows - 1]
    earliest_key = jnp.min(first_key)

    def visible_mask(start_row, length):
        key_pos = start_row + jnp.arange(length, dtype=jnp.int32)
        return (key_pos[None, :] <= query_pos[:, None]) & (key_pos[None, :] >= first_key[:, None])

    def reachable(start_row, length):
        return (start_row <= last_query) & (start_row + length - 1 >= earliest_key)

    def attend_block(running, key_block, value_block, start_row):
        row_max, row_sum, accumulated = running
        visible = visible_mask(start_row, key_block.shape[0])
        scores = (
            jnp.einsum("qhd,khd->hqk", queries, key_block, preferred_element_type=jnp.float32)
            * score_scale
        )
        scores = jnp.where(visible[None], scores, -1e30)
        new_max = jnp.maximum(row_max, jnp.max(scores, axis=-1))
        weights = jnp.where(visible[None], jnp.exp(scores - new_max[..., None]), 0.0)
        factor = jnp.exp(row_max - new_max)
        row_sum = row_sum * factor + jnp.sum(weights, axis=-1)
        accumulated = accumulated * factor[..., None] + jnp.einsum(
            "hqk,khd->hqd",
            weights.astype(jnp.bfloat16),
            value_block,
            preferred_element_type=jnp.float32,
        )
        return (new_max, row_sum, accumulated)

    initial = (
        jnp.full((head_count, block_rows), -1e30, jnp.float32),
        jnp.zeros((head_count, block_rows), jnp.float32),
        jnp.zeros((head_count, block_rows, HD), jnp.float32),
    )
    running = initial
    key_rows = lax.all_gather(keys_rot, "ctx", axis=0, tiled=True)
    value_rows = lax.all_gather(values, "ctx", axis=0, tiled=True)
    length = key_rows.shape[0]
    attend_step_rows = block_length(length)
    steps_count = length // attend_step_rows
    key_blocks = key_rows.reshape(steps_count, attend_step_rows, head_count, HD)
    value_blocks = value_rows.reshape(steps_count, attend_step_rows, head_count, HD)

    def one_step(current, inputs_step):
        key_block, value_block, number = inputs_step
        block_start = number * attend_step_rows

        def attend_now(state):
            return attend_block(state, key_block, value_block, block_start)

        def keep_state(state):
            return state

        return (
            lax.cond(reachable(block_start, attend_step_rows), attend_now, keep_state, current),
            None,
        )

    running, unused = lax.scan(
        one_step, running, (key_blocks, value_blocks, jnp.arange(steps_count, dtype=jnp.int32))
    )
    row_max, row_sum, accumulated = running
    attended = jnp.transpose(accumulated / row_sum[..., None], (1, 0, 2)).astype(jnp.bfloat16)
    log_total = row_max + jnp.log(row_sum)
    attended_flat = attended.reshape(block_rows, local_width)
    attn_part = jnp.dot(attended_flat, dense_weight, preferred_element_type=jnp.float32)
    pre_act = jnp.dot(mlp_in, up_weight, preferred_element_type=jnp.float32) + up_bias
    activation = jax.nn.gelu(pre_act, approximate=False).astype(jnp.bfloat16)
    mlp_part = jnp.dot(activation, down_weight, preferred_element_type=jnp.float32)
    branch_sum = lax.psum_scatter(attn_part + mlp_part, "tp", scatter_dimension=0, tiled=True)
    output = (resid + branch_sum + dense_bias + down_bias).astype(jnp.bfloat16)
    grad_out = cotangent.astype(jnp.float32)
    bias_grad = jnp.sum(grad_out, axis=0)
    grad_full = lax.all_gather(cotangent, "tp", axis=0, tiled=True)
    grad_down = jnp.dot(activation.T, grad_full, preferred_element_type=jnp.float32)
    grad_act = jnp.dot(grad_full, down_weight.T, preferred_element_type=jnp.float32)
    grad_pre = grad_act * gelu_grad(pre_act)
    grad_up_bias = jnp.sum(grad_pre, axis=0)
    grad_pre_low = grad_pre.astype(jnp.bfloat16)
    grad_up = jnp.dot(mlp_in.T, grad_pre_low, preferred_element_type=jnp.float32)
    grad_mlp_in = jnp.dot(grad_pre_low, up_weight.T, preferred_element_type=jnp.float32)
    grad_dense = jnp.dot(attended_flat.T, grad_full, preferred_element_type=jnp.float32)
    grad_attended = jnp.dot(grad_full, dense_weight.T, preferred_element_type=jnp.float32)
    grad_attended = grad_attended.astype(jnp.bfloat16).reshape(block_rows, head_count, HD)
    delta_rows = jnp.transpose(
        jnp.sum(grad_attended.astype(jnp.float32) * attended.astype(jnp.float32), axis=-1)
    )

    def score_grads(query_rows, grad_rows, log_rows, delta_part, key_block, value_block, visible):
        scores = (
            jnp.einsum("qhd,khd->hqk", query_rows, key_block, preferred_element_type=jnp.float32)
            * score_scale
        )
        weights = jnp.where(visible[None], jnp.exp(scores - log_rows[..., None]), 0.0)
        grad_weights = jnp.einsum(
            "qhd,khd->hqk", grad_rows, value_block, preferred_element_type=jnp.float32
        )
        grad_scores = (weights * (grad_weights - delta_part[..., None])).astype(jnp.bfloat16)
        return (weights.astype(jnp.bfloat16), grad_scores)

    key_back, value_back = (
        lax.all_gather(keys_rot, "ctx", axis=0, tiled=True),
        lax.all_gather(values, "ctx", axis=0, tiled=True),
    )
    total_rows = key_back.shape[0]
    step_rows = block_length(total_rows)
    steps_count = total_rows // step_rows
    back_inputs = (
        key_back.reshape(steps_count, step_rows, head_count, HD),
        value_back.reshape(steps_count, step_rows, head_count, HD),
        jnp.arange(steps_count, dtype=jnp.int32),
    )
    zero_query = jnp.zeros((block_rows, head_count, HD), jnp.float32)

    def back_step(query_grad, inputs_step):
        key_block, value_block, number = inputs_step
        block_start = number * step_rows

        def with_terms(grad_now):
            visible = visible_mask(block_start, step_rows)
            weights_low, grad_scores = score_grads(
                queries, grad_attended, log_total, delta_rows, key_block, value_block, visible
            )
            grad_now = (
                grad_now
                + jnp.einsum(
                    "hqk,khd->qhd", grad_scores, key_block, preferred_element_type=jnp.float32
                )
                * score_scale
            )
            key_part = (
                jnp.einsum("hqk,qhd->khd", grad_scores, queries, preferred_element_type=jnp.float32)
                * score_scale
            )
            value_part = jnp.einsum(
                "hqk,qhd->khd", weights_low, grad_attended, preferred_element_type=jnp.float32
            )
            joined = jnp.concatenate(
                [
                    key_part.reshape(step_rows, local_width),
                    value_part.reshape(step_rows, local_width),
                ],
                axis=1,
            )
            return (grad_now, joined)

        def without_terms(grad_now):
            return (grad_now, jnp.zeros((step_rows, 2 * local_width), jnp.float32))

        return lax.cond(reachable(block_start, step_rows), with_terms, without_terms, query_grad)

    query_grad, key_terms = lax.scan(back_step, zero_query, back_inputs)
    key_terms = key_terms.reshape(total_rows, 2 * local_width)
    own_terms = lax.psum_scatter(key_terms, "ctx", scatter_dimension=0, tiled=True)
    key_grad = own_terms[:, :local_width].reshape(block_rows, head_count, HD)
    value_grad = own_terms[:, local_width:].reshape(block_rows, head_count, HD)
    grad_query_pre = rotate(query_grad, cosines, -sines)
    grad_key_pre = rotate(key_grad, cosines, -sines)
    qv_bias_grad = jnp.stack(
        [
            jnp.sum(grad_query_pre, axis=0).reshape(local_width),
            jnp.sum(value_grad, axis=0).reshape(local_width),
        ]
    )
    grad_proj = jnp.stack([grad_query_pre, grad_key_pre, value_grad], axis=1)
    grad_proj = grad_proj.reshape(block_rows, 3 * local_width).astype(jnp.bfloat16)
    grad_qkv = jnp.dot(attn_in.T, grad_proj, preferred_element_type=jnp.float32).reshape(
        D, 3, local_width
    )
    grad_attn_in = jnp.dot(
        grad_proj, qkv_weight.reshape(D, 3 * local_width).T, preferred_element_type=jnp.float32
    )
    own_attn, own_mlp = (
        lax.psum_scatter(grad_attn_in, "tp", scatter_dimension=0, tiled=True),
        lax.psum_scatter(grad_mlp_in, "tp", scatter_dimension=0, tiled=True),
    )
    grad_input = grad_out + norm_backward(own_attn, hat_one, std_one, attn_scale)
    grad_input = grad_input + norm_backward(own_mlp, hat_two, std_two, mlp_scale)
    norm_sums = lax.psum(
        (
            jnp.sum(own_attn * hat_one, axis=0),
            jnp.sum(own_attn, axis=0),
            jnp.sum(own_mlp * hat_two, axis=0),
            jnp.sum(own_mlp, axis=0),
            bias_grad,
        ),
        ("ctx", "tp"),
    )
    weight_sums = lax.psum(
        (grad_qkv, qv_bias_grad, grad_dense, grad_up, grad_up_bias, grad_down), "ctx"
    )
    return (
        output,
        grad_input,
        norm_sums[0],
        norm_sums[1],
        norm_sums[2],
        norm_sums[3],
        weight_sums[0],
        weight_sums[1],
        weight_sums[2],
        norm_sums[4],
        weight_sums[3],
        weight_sums[4],
        weight_sums[5],
        norm_sums[4],
    )


def solution(mesh):
    in_specs = (
        P(("ctx", "tp"), None),
        P("ctx"),
        P(),
        P(),
        P(),
        P(),
        P(None, None, "tp"),
        P(None, "tp"),
        P("tp", None),
        P(),
        P(None, "tp"),
        P("tp"),
        P("tp", None),
        P(),
        P(("ctx", "tp"), None),
    )
    out_specs = (
        P(("ctx", "tp"), None),
        P(("ctx", "tp"), None),
        P(),
        P(),
        P(),
        P(),
        P(None, None, "tp"),
        P(None, "tp"),
        P("tp", None),
        P(),
        P(None, "tp"),
        P("tp"),
        P("tp", None),
        P(),
    )
    return jax.shard_map(local, mesh=mesh, in_specs=in_specs, out_specs=out_specs, check_vma=False)
```

profile of v0, /device:TPU:0, one launch (start us, length us, event | category | flops | bytes accessed | tf_op | source)
XLA Modules:
  0.0 690.6 jit_solution(9488253124478135631)
XLA Ops:
  9.6 1.9 fusion.74
  11.5 10.1 %all_gather.17 = bf16[512,768]{1,0:T(8,128)(2,1)S(1)} all-gather(bf16[128,768]{1,0:T(8,128)(2,1)S(1)} %get-tuple-element.958), channel_id=1, replica_groups=mesh['ctx'=8,'tp'=4] {'tp'}, dimensions={0}, use_global_device_ids=true | all-gather | bytes 983040 | tf_op jit(solution)/shard_map/all_gather | solution.py:78
  27.7 8.7 %all_gather.21 = bf16[512,768]{1,0:T(8,128)(2,1)S(1)} all-gather(bf16[128,768]{1,0:T(8,128)(2,1)S(1)} %copy-done.29), channel_id=1, replica_groups=mesh['ctx'=8,'tp'=4] {'tp'}, dimensions={0}, use_global_device_ids=true | all-gather | bytes 983040 | tf_op jit(solution)/shard_map/all_gather | solution.py:169
  37.7 33.9 %all-gather.3.cloned.1.call-done = bf16[4096,3,64]{0,2,1:T(8,128)(2,1)} async-done(((bf16[512,3,64]{0,2,1:T(8,128)(2,1)}), bf16[4096,3,64]{0,2,1:T(8,128)(2,1)}) %all-gather.3.cloned.1.call-update) | async-done | bytes 1572880 | tf_op jit(solution)/shard_map/all_gather | solution.py:131
  73.2 43.7 %all-gather.5.cloned.1.call-done = bf16[4096,3,64]{0,2,1:T(8,128)(2,1)} async-done(((bf16[512,3,64]{0,2,1:T(8,128)(2,1)}), bf16[4096,3,64]{0,2,1:T(8,128)(2,1)}) %all-gather.5.cloned.1.call-update) | async-done | bytes 1572880 | tf_op jit(solution)/shard_map/all_gather | solution.py:132
  116.9 2.7 copy.74
  120.1 23.0 %while.39 = (s32[]{:T(128)}, f32[3,512]{1,0:T(4,128)S(1)}, f32[3,512]{1,0:T(4,128)S(1)}, f32[3,512,64]{1,2,0:T(8,128)S(1)}, s32[4]{0:T(128)}, /*index=5*/s32[]{:...) while((s32[]{:T(128)}, f32[3,512]{1,0:T(4,128)S(1)}, ...), condition=%wide.region_8.9_spmd.clone, body=%wide.region_3.8_spmd.clone.sunk | while | flops 424874496 | bytes 22858608 | solution.py:154
  123.9 7.8 %conditional.6 = ((f32[3,512]{1,0:T(4,128)S(1)}, f32[3,512]{1,0:T(4,128)S(1)}, f32[3,512,64]{1,2,0:T(8,128)S(1)})) conditional(s32[]{:T(128)} %convert_element_type.207, (f32[3,512]{1,0:T(4,128)S(1)}, f32[3,512]{1,0:T(4,128)S(1)}, f32[3,512,64]{1,2,0:T(8,128)S(1)}) %tuple.156, (s32[]{:T(128)}, s32[]{:T(128)}, s32[512]{0:T(512)}, ...), branch_computations={%region_4.4_spmd, %region_5.7_spmd} | conditional | flops 424874496 | bytes 22856236 | solution.py:150
  128.8 3.0 fusion.10
  145.1 37.2 %while.40 = (s32[]{:T(128)}, f32[512,3,64]{0,2,1:T(8,128)S(1)}, f32[4,1024,384]{2,1,0:T(8,128)}, s32[4]{0:T(128)S(1)}, s32[]{:T(128)}, /*index=5*/s32[]{:T(128)}...) while((s32[]{:T(128)}, f32[512,3,64]{0,2,1:T(8,128)S(1)}, ...), condition=%wide.region_14.15_spmd.clone, body=%wide.region_11.14_spmd.clone.sunk | while | flops 1024722432 | bytes 56325616 | solution.py:247
  147.8 8.3 %conditional.7 = (f32[512,3,64]{0,2,1:T(8,128)S(1)}, f32[1,1024,384]{1,2,0:T(8,128)S(1)}) conditional(s32[]{:T(128)} %convert_element_type.208, f32[512,3,64]{0,2,1:T(8,128)S(1)} %get-tuple-element.1217, (s32[]{:T(128)}, s32[]{:T(128)}, s32[512]{0:T(512)}, bf16[4,1024,3,64]{1,3,2,0:T(8,128)(2,1)S(1)}, s32[]{:T(128)}, ...), branch_computations={%region_12.12_spmd, %region_13.13_spmd} | conditional | flops 1024722432 | bytes 37448308 | solution.py:245
  149.4 3.3 fusion.23
  157.7 2.8 constant_dynamic-update-slice_fusion.2
  165.0 2.8 constant_dynamic-update-slice_fusion.2
  172.3 2.8 constant_dynamic-update-slice_fusion.2
  179.5 2.8 constant_dynamic-update-slice_fusion.2
  183.3 8.7 %all_gather.20 = bf16[512,768]{1,0:T(8,128)(2,1)S(1)} all-gather(bf16[128,768]{1,0:T(8,128)(2,1)S(1)} %copy-done.31), channel_id=1, replica_groups=mesh['ctx'=8,'tp'=4] {'tp'}, dimensions={0}, use_global_device_ids=true | all-gather | bytes 983040 | tf_op jit(solution)/shard_map/all_gather | solution.py:79
  192.0 4.2 fusion.44
  198.3 2.0 fusion.93
  201.8 144.9 %reduce-scatter.7.cloned.1.call-done = f32[512,384]{1,0:T(8,128)} async-done(((f32[4096,384]{1,0:T(8,128)}), f32[512,384]{1,0:T(8,128)}) %reduce-scatter.7.cloned.1.call-update) | async-done | bytes 786448 | tf_op jit(solution)/shard_map/reduce_scatter | solution.py:249
  346.7 2.0 slice.122
  354.5 2.0 fusion.111
  357.9 2.0 convolution_add_fusion
  361.0 3.3 fusion.91
  364.4 2.2 fusion.113
  371.1 20.6 %all-reduce.1 = (f32[2,192]{1,0:T(2,128)}, f32[768]{0:T(1024)}) all-reduce(f32[2,192]{1,0:T(2,128)S(1)} %pad_maximum_fusion.4, f32[768]{0:T(1024)S(1)} %get-tuple-element.970), channel_id=1, replica_groups=mesh['ctx'=8,'tp'=4] {'ctx'}, use_global_device_ids=true, to_apply=%region_33.34 | all-reduce | flops 1152 | bytes 9216 | tf_op jit(solution)/shard_map/psum | solution.py:284
  391.7 15.1 %reduce-scatter.9.cloned.1.call-done = f32[128,768]{1,0:T(8,128)} async-done(((f32[512,768]{1,0:T(8,128)}), f32[128,768]{1,0:T(8,128)}) %reduce-scatter.9.cloned.1.call-update) | async-done | bytes 393232 | tf_op jit(solution)/shard_map/reduce_scatter | solution.py:269
  408.3 28.8 %reduce-scatter.5.cloned.1.call-done = f32[128,768]{1,0:T(8,128)} async-done(((f32[512,768]{1,0:T(8,128)}), f32[128,768]{1,0:T(8,128)}) %reduce-scatter.5.cloned.1.call-update) | async-done | bytes 393232 | tf_op jit(solution)/shard_map/reduce_scatter | solution.py:165
  437.2 2.3 convert_reduce_fusion.1
  439.5 43.0 %all-reduce = (f32[768]{0:T(1024)}, f32[768]{0:T(1024)}, f32[768]{0:T(1024)}, f32[768]{0:T(1024)}, f32[768]{0:T(1024)S(1)}) all-reduce(f32[768]{0:T(1024)S(1)} %get-tuple-element.862, f32[768]{0:T(1024)S(1)} %get-tuple-element.867, f32[768]{0:T(1024)S(1)} %get-tuple-element.871, ...), channel_id=1, replica_groups=mesh['ctx'=8,'tp'=4] {'ctx','tp'}, use_global_device_ids=true, to_apply=%region_23.24 | all-reduce | flops 3840 | bytes 30720 | tf_op jit(solution)/shard_map/psum | solution.py:274
  482.5 193.0 %all-reduce.5.cloned.1.call-done = (f32[768,3,192]{0,2,1:T(8,128)}, f32[192,768]{1,0:T(8,128)}, f32[768,768]{1,0:T(8,128)}, f32[768,768]{1,0:T(8,128)}) async-done(((f32[768,3,192]{0,2,1:T(8,128)}, f32[192,768]{1,0:T(8,128)}, f32[768,768]{1,0:T(8,128)}, f32[768,768]{1,0:T(8,128)}), (f32[768,3,192]{0,2,1:T(8,128)}, f32[192,768]{1,0:T(8,128)}, f32[768,768]{1,0:T(8,128)}, ...) | async-done | bytes 7077904 | tf_op jit(solution)/shard_map/psum | solution.py:284
  676.0 2.9 copy.118
  (237 shorter events, 65.0 us)
Async XLA Ops:
  7.2 184.8 %copy-start = (bf16[768,768]{1,0:T(8,128)(2,1)S(1)}, bf16[768,768]{1,0:T(8,128)(2,1)}, u32[]{:S(2)}) copy-start(bf16[768,768]{1,0:T(8,128)(2,1)} %param.33) | copy-start | bytes 3538948
  7.2 14.4 %copy-start.12 = (bf16[768,3,192]{0,2,1:T(8,128)(2,1)S(1)}, bf16[768,3,192]{0,2,1:T(8,128)(2,1)}, u32[]{:S(2)}) copy-start(bf16[768,3,192]{0,2,1:T(8,128)(2,1)} %param.29) | copy-start | bytes 2654212
  7.2 64.4 %all-gather.3.cloned.1.call-start = ((), (), s32[]{:S(2)}) async-start(), calls=%async_computation.4 | async-start | bytes 1769472 | tf_op jit(solution)/shard_map/all_gather | solution.py:131
  8.5 13.1 %copy-start.41 = (f32[128]{0:T(128)}, f32[128]{0:T(128)S(1)}, u32[]{:S(2)}) copy-start(f32[128]{0:T(128)S(1)} %broadcast_multiply_fusion.5) | copy-start | bytes 1540
  9.6 12.0 %copy-start.44 = (f32[128]{0:T(128)}, f32[128]{0:T(128)S(1)}, u32[]{:S(2)}) copy-start(f32[128]{0:T(128)S(1)} %add_rsqrt_fusion) | copy-start | bytes 1540
  23.5 4.2 copy-start.29
  24.8 12.5 %copy-start.23 = (bf16[192,768]{1,0:T(8,128)(2,1)S(1)}, bf16[192,768]{1,0:T(8,128)(2,1)}, u32[]{:S(2)}) copy-start(bf16[192,768]{1,0:T(8,128)(2,1)} %param.31) | copy-start | bytes 884740
  25.5 12.2 %copy-start.34 = (f32[512,16]{0,1:T(8,128)}, f32[512,16]{0,1:T(8,128)S(1)}, u32[]{:S(2)}) copy-start(f32[512,16]{0,1:T(8,128)S(1)} %get-tuple-element.966) | copy-start | bytes 98308
  26.2 90.6 %all-gather.5.cloned.1.call-start = ((), (), s32[]{:S(2)}) async-start(), calls=%async_computation.5 | async-start | bytes 1769472 | tf_op jit(solution)/shard_map/all_gather | solution.py:132
  27.0 319.7 %reduce-scatter.7.cloned.1.call-start = ((), (), s32[]{:S(2)}) async-start(), calls=%async_computation.7 | async-start | bytes 7077888 | tf_op jit(solution)/shard_map/reduce_scatter | solution.py:249
  157.7 2.8 copy-start.2
  179.5 2.8 copy-start.2
  182.3 9.7 %copy-start.51 = (f32[768]{0:T(1024)S(1)}, f32[768]{0:T(1024)}, u32[]{:S(2)}) copy-start(f32[768]{0:T(1024)} %param.34) | copy-start | bytes 9220
  182.4 209.3 %reduce-scatter.11.cloned.1.call-start = ((), (), s32[]{:S(2)}) async-start(), calls=%async_computation.9 | async-start | bytes 1966080 | tf_op jit(solution)/shard_map/reduce_scatter | solution.py:270
  192.0 4.3 copy-start.7
  192.0 4.3 copy-start.4
  192.0 4.3 copy-start.21
  200.3 206.5 %reduce-scatter.9.cloned.1.call-start = ((), (), s32[]{:S(2)}) async-start(), calls=%async_computation.8 | async-start | bytes 1966080 | tf_op jit(solution)/shard_map/reduce_scatter | solution.py:269
  346.7 3.7 copy-start.18
  356.5 80.7 %reduce-scatter.5.cloned.1.call-start = ((), (), s32[]{:S(2)}) async-start(), calls=%async_computation.6 | async-start | bytes 1966080 | tf_op jit(solution)/shard_map/reduce_scatter | solution.py:165
  359.9 315.5 %all-reduce.5.cloned.1.call-start = ((), (), s32[]{:S(2)}) async-start(), calls=%async_computation.10 | async-start | bytes 14155776 | tf_op jit(solution)/shard_map/psum | solution.py:284
  369.9 36.9 %copy-start.11 = (bf16[128,768]{1,0:T(8,128)(2,1)S(1)}, bf16[128,768]{1,0:T(8,128)(2,1)}, u32[]{:S(2)}) copy-start(bf16[128,768]{1,0:T(8,128)(2,1)} %param.23) | copy-start | bytes 589828
  369.9 36.9 %copy-start.38 = (f32[768]{0:T(1024)S(1)}, f32[768]{0:T(1024)}, u32[]{:S(2)}) copy-start(f32[768]{0:T(1024)} %param.27) | copy-start | bytes 9220
  369.9 36.9 %copy-start.39 = (f32[768]{0:T(1024)S(1)}, f32[768]{0:T(1024)}, u32[]{:S(2)}) copy-start(f32[768]{0:T(1024)} %param.25) | copy-start | bytes 9220
  369.9 36.9 %copy-start.42 = (f32[128]{0:T(128)S(1)}, f32[128]{0:T(128)}, u32[]{:S(2)}) copy-start(f32[128]{0:T(128)} %copy-done.41) | copy-start | bytes 1540
  369.9 36.9 %copy-start.45 = (f32[128]{0:T(128)S(1)}, f32[128]{0:T(128)}, u32[]{:S(2)}) copy-start(f32[128]{0:T(128)} %copy-done.44) | copy-start | bytes 1540
  369.9 67.2 %copy-start.46 = (f32[768]{0:T(1024)S(1)}, f32[768]{0:T(1024)}, u32[]{:S(2)}) copy-start(f32[768]{0:T(1024)} %param.36) | copy-start | bytes 9220
  369.9 67.2 %copy-start.47 = (f32[768]{0:T(1024)S(1)}, f32[768]{0:T(1024)}, u32[]{:S(2)}) copy-start(f32[768]{0:T(1024)} %param.32) | copy-start | bytes 9220
  370.9 66.3 %copy-start.30 = (bf16[128,768]{1,0:T(8,128)(2,1)S(1)}, bf16[128,768]{1,0:T(8,128)(2,1)}, u32[]{:S(2)}) copy-start(bf16[128,768]{1,0:T(8,128)(2,1)} %param.37) | copy-start | bytes 589828
  482.5 196.5 %copy-start.48 = (f32[768]{0:T(1024)}, f32[768]{0:T(1024)S(1)}, u32[]{:S(2)}) copy-start(f32[768]{0:T(1024)S(1)} %get-tuple-element.1287) | copy-start | bytes 9220
  676.0 3.0 copy-start.33
  676.0 3.8 copy-start.17
  (33 other events, 52.1 us)
Sparse Core Ops, SparseCore 0:
  26.3 45.2 all-gather.2
  74.2 42.5 all-gather.4
  182.5 164.1 reduce-scatter.6
  349.1 27.2 reduce-scatter.10
  378.7 27.9 reduce-scatter.8
  409.2 27.9 reduce-scatter.4
  442.7 232.6 all-reduce.4
where the time goes:
time: 692 us; the launch traced here: 691 us
  waiting for transfers between devices  460 us (66%)
  blocking collectives  91.1 us (13%)
  local copies, waits for them, and re-layouts  54.8 us (8%)
  matrix products  33.3 us (5%)
  other arithmetic  20.3 us (3%)
  loops' own time  16 us (2%)
  between operations  14.7 us (2%)
    psum x1, waiting for transfers between devices, local(): lax.psum((grad_qkv, qv_bias_grad, grad_dense, grad_up, grad_up_bias, grad...  193 us
    reduce_scatter x1, waiting for transfers between devices, local(): lax.psum_scatter(key_terms, 'ctx', scatter_dimension=0, tiled=True)  145 us
    all_gather x1, waiting for transfers between devices, local(): value_rows = lax.all_gather(values, 'ctx', axis=0, tiled=True)  43.7 us
    psum x1, blocking collectives, local(): lax.psum((jnp.sum(own_attn * hat_one, axis=0), jnp.sum(own_attn, axis=0),...  43 us
    all_gather x1, waiting for transfers between devices, local(): key_rows = lax.all_gather(keys_rot, 'ctx', axis=0, tiled=True)  33.9 us
    reduce_scatter x1, waiting for transfers between devices, local(): lax.psum_scatter(attn_part + mlp_part, 'tp', scatter_dimension=0, tiled=T...  28.8 us
    psum x1, blocking collectives, local(): lax.psum((grad_qkv, qv_bias_grad, grad_dense, grad_up, grad_up_bias, grad...  20.6 us
    dynamic_update_slice x8, local copies, waits for them, and re-layouts, local(): query_grad, key_terms = lax.scan(back_step, zero_query, back_inputs)  17.6 us
  transfers between devices with their start and end apart: 7, of which 6 were waited for; matrix products, arithmetic and copies ran while one was open for 5% of the time, Pallas kernels for 0%

commit v1 on v0

--- a/solution.py
+++ b/solution.py
@@ -128,8 +128,11 @@
         jnp.zeros((head_count, block_rows, HD), jnp.float32),
     )
     running = initial
-    key_rows = lax.all_gather(keys_rot, "ctx", axis=0, tiled=True)
-    value_rows = lax.all_gather(values, "ctx", axis=0, tiled=True)
+    key_rows, value_rows = jnp.split(
+        lax.all_gather(jnp.concatenate([keys_rot, values], axis=1), "ctx", axis=0, tiled=True),
+        [keys_rot.shape[1]],
+        axis=1,
+    )
     length = key_rows.shape[0]
     attend_step_rows = block_length(length)
     steps_count = length // attend_step_rows

time: 692 us -> 754 us (1.090)
  waiting for transfers between devices: 460 us -> 521 us
    all_gather x2 -> x3, waiting for transfers between devices: 77.6 us -> 136 us  [the longest x1 60.8 us: local(): lax.all_gather(jnp.concatenate([keys_rot, values], axis=1), 'ctx', axis=0...]
    unnamed x99 -> x89, local copies, waits for them, and re-layouts: 15.8 us -> 14.7 us
  transfers between devices with their start and end apart: 7 -> 8, of which waited for: 6 -> 7; matrix products, arithmetic and copies ran while one was open for 5% -> 5% of each run, Pallas kernels for 0% -> 0%
where the time goes in v1:
time: 754 us; the launch traced here: 752 us
  waiting for transfers between devices  521 us (69%)
  blocking collectives  91.2 us (12%)
  local copies, waits for them, and re-layouts  50.5 us (7%)
  matrix products  36.6 us (5%)
  other arithmetic  21.9 us (3%)
  loops' own time  16.4 us (2%)
  between operations  14.6 us (2%)
    psum x1, waiting for transfers between devices, local(): lax.psum((grad_qkv, qv_bias_grad, grad_dense, grad_up, grad_up_bias, grad...  193 us
    reduce_scatter x1, waiting for transfers between devices, local(): lax.psum_scatter(key_terms, 'ctx', scatter_dimension=0, tiled=True)  147 us
    all_gather x1, waiting for transfers between devices, local(): lax.all_gather(jnp.concatenate([keys_rot, values], axis=1), 'ctx', axis=0...  60.8 us
    psum x1, blocking collectives, local(): lax.psum((jnp.sum(own_attn * hat_one, axis=0), jnp.sum(own_attn, axis=0),...  43 us
    all_gather x1, waiting for transfers between devices, local(): lax.all_gather(values, 'ctx', axis=0, tiled=True)  42.5 us
    all_gather x1, waiting for transfers between devices, local(): lax.all_gather(keys_rot, 'ctx', axis=0, tiled=True)  32.3 us
    reduce_scatter x1, waiting for transfers between devices, local(): lax.psum_scatter(attn_part + mlp_part, 'tp', scatter_dimension=0, tiled=T...  29 us
    psum x1, blocking collectives, local(): lax.psum((grad_qkv, qv_bias_grad, grad_dense, grad_up, grad_up_bias, grad...  20.8 us
  transfers between devices with their start and end apart: 8, of which 7 were waited for; matrix products, arithmetic and copies ran while one was open for 5% of the time, Pallas kernels for 0%

profile of v1, /device:TPU:0, one launch (start us, length us, event | category | flops | bytes accessed | tf_op | source)
XLA Modules:
  0.0 752.2 jit_solution(12467034180665352706)
XLA Ops:
  11.9 10.1 %all_gather.18 = bf16[512,768]{1,0:T(8,128)(2,1)S(1)} all-gather(bf16[128,768]{1,0:T(8,128)(2,1)S(1)} %get-tuple-element.960), channel_id=1, replica_groups=mesh['ctx'=8,'tp'=4] {'tp'}, dimensions={0}, use_global_device_ids=true | all-gather | bytes 983040 | tf_op jit(solution)/shard_map/all_gather | solution.py:78
  28.4 8.7 %all_gather.23 = bf16[512,768]{1,0:T(8,128)(2,1)S(1)} all-gather(bf16[128,768]{1,0:T(8,128)(2,1)S(1)} %copy-done.24), channel_id=1, replica_groups=mesh['ctx'=8,'tp'=4] {'tp'}, dimensions={0}, use_global_device_ids=true | all-gather | bytes 983040 | tf_op jit(solution)/shard_map/all_gather | solution.py:172
  39.1 32.3 %all-gather.6.cloned.1.call-done = bf16[4096,3,64]{0,2,1:T(8,128)(2,1)} async-done(((bf16[512,3,64]{0,2,1:T(8,128)(2,1)}), bf16[4096,3,64]{0,2,1:T(8,128)(2,1)}) %all-gather.6.cloned.1.call-update) | async-done | bytes 1572880 | tf_op jit(solution)/shard_map/all_gather | solution.py:200
  71.4 2.7 copy.79
  74.1 42.5 %all-gather.8.cloned.1.call-done = bf16[4096,3,64]{0,2,1:T(8,128)(2,1)} async-done(((bf16[512,3,64]{0,2,1:T(8,128)(2,1)}), bf16[4096,3,64]{0,2,1:T(8,128)(2,1)}) %all-gather.8.cloned.1.call-update) | async-done | bytes 1572880 | tf_op jit(solution)/shard_map/all_gather | solution.py:201
  116.7 2.7 copy.78
  119.4 60.8 %all-gather.4.cloned.1.call-done = bf16[4096,6,64]{0,2,1:T(8,128)(2,1)} async-done(((bf16[512,6,64]{0,2,1:T(8,128)(2,1)}), bf16[4096,6,64]{0,2,1:T(8,128)(2,1)}) %all-gather.4.cloned.1.call-update) | async-done | bytes 3145744 | tf_op jit(solution)/shard_map/all_gather | solution.py:132
  180.1 2.2 fusion.109
  183.9 17.0 %while.39 = (s32[]{:T(128)}, f32[3,512]{1,0:T(4,128)S(1)}, f32[3,512]{1,0:T(4,128)S(1)}, f32[3,512,64]{1,2,0:T(8,128)S(1)}, s32[4]{0:T(128)S(1)}, /*index=5*/s32...) while((s32[]{:T(128)}, f32[3,512]{1,0:T(4,128)S(1)}, ...), condition=%wide.region_8.9_spmd.clone, body=%wide.region_3.8_spmd.clone.sunk | while | flops 424874496 | bytes 22858608 | solution.py:157
  186.6 6.5 conditional.6
  190.2 3.0 fusion.10
  203.2 38.5 %while.40 = (s32[]{:T(128)}, f32[512,3,64]{0,2,1:T(8,128)S(1)}, f32[4,1024,384]{2,1,0:T(8,128)}, s32[4]{0:T(128)S(1)}, s32[]{:T(128)}, /*index=5*/s32[]{:T(128)}...) while((s32[]{:T(128)}, f32[512,3,64]{0,2,1:T(8,128)S(1)}, ...), condition=%wide.region_14.15_spmd.clone, body=%wide.region_11.14_spmd.clone.sunk | while | flops 1024722432 | bytes 44522088 | solution.py:250
  205.8 10.4 %conditional.7 = (f32[512,3,64]{0,2,1:T(8,128)S(1)}, f32[1,1024,384]{1,2,0:T(8,128)S(1)}) conditional(s32[]{:T(128)} %convert_element_type.208, f32[512,3,64]{0,2,1:T(8,128)S(1)} %get-tuple-element.1219, (s32[]{:T(128)}, s32[]{:T(128)}, s32[512]{0:T(512)S(1)}, bf16[4,1024,3,64]{1,3,2,0:T(8,128)(2,1)}, s32[]{:T(128)}, ...), branch_computations={%region_12.12_spmd, %region_13.13_spmd} | conditional | flops 1024722432 | bytes 38227564 | solution.py:248
  205.8 2.1 fusion.32
  208.4 3.3 fusion.23
  217.8 2.7 constant_dynamic-update-slice_fusion.2
  224.9 2.7 constant_dynamic-update-slice_fusion.2
  231.9 2.7 constant_dynamic-update-slice_fusion.2
  239.0 2.7 constant_dynamic-update-slice_fusion.2
  242.6 8.6 %all_gather.20 = bf16[512,768]{1,0:T(8,128)(2,1)S(1)} all-gather(bf16[128,768]{1,0:T(8,128)(2,1)S(1)} %copy-done.26), channel_id=1, replica_groups=mesh['ctx'=8,'tp'=4] {'tp'}, dimensions={0}, use_global_device_ids=true | all-gather | bytes 983040 | tf_op jit(solution)/shard_map/all_gather | solution.py:79
  251.3 4.5 fusion.44
  261.3 146.8 %reduce-scatter.7.cloned.1.call-done = f32[512,384]{1,0:T(8,128)} async-done(((f32[4096,384]{1,0:T(8,128)}), f32[512,384]{1,0:T(8,128)}) %reduce-scatter.7.cloned.1.call-update) | async-done | bytes 786448 | tf_op jit(solution)/shard_map/reduce_scatter | solution.py:252
  410.2 2.2 slice_reduce_fusion.2
  421.8 3.6 fusion.91
  425.4 2.2 fusion.114
  432.1 20.8 %all-reduce.1 = (f32[2,192]{1,0:T(2,128)}, f32[768]{0:T(1024)}) all-reduce(f32[2,192]{1,0:T(2,128)S(1)} %pad_maximum_fusion.5, f32[768]{0:T(1024)S(1)} %get-tuple-element.972), channel_id=1, replica_groups=mesh['ctx'=8,'tp'=4] {'ctx'}, use_global_device_ids=true, to_apply=%region_33.34 | all-reduce | flops 1152 | bytes 9216 | tf_op jit(solution)/shard_map/psum | solution.py:287
  452.8 15.4 %reduce-scatter.9.cloned.1.call-done = f32[128,768]{1,0:T(8,128)} async-done(((f32[512,768]{1,0:T(8,128)}), f32[128,768]{1,0:T(8,128)}) %reduce-scatter.9.cloned.1.call-update) | async-done | bytes 393232 | tf_op jit(solution)/shard_map/reduce_scatter | solution.py:272
  469.8 29.0 %reduce-scatter.5.cloned.1.call-done = f32[128,768]{1,0:T(8,128)} async-done(((f32[512,768]{1,0:T(8,128)}), f32[128,768]{1,0:T(8,128)}) %reduce-scatter.5.cloned.1.call-update) | async-done | bytes 393232 | tf_op jit(solution)/shard_map/reduce_scatter | solution.py:168
  498.8 2.3 convert_reduce_fusion.1
  501.1 43.0 %all-reduce = (f32[768]{0:T(1024)}, f32[768]{0:T(1024)}, f32[768]{0:T(1024)}, f32[768]{0:T(1024)}, f32[768]{0:T(1024)S(1)}) all-reduce(f32[768]{0:T(1024)S(1)} %get-tuple-element.862, f32[768]{0:T(1024)S(1)} %get-tuple-element.867, f32[768]{0:T(1024)S(1)} %get-tuple-element.871, ...), channel_id=1, replica_groups=mesh['ctx'=8,'tp'=4] {'ctx','tp'}, use_global_device_ids=true, to_apply=%region_23.24 | all-reduce | flops 3840 | bytes 30720 | tf_op jit(solution)/shard_map/psum | solution.py:277
  544.1 192.9 %all-reduce.5.cloned.1.call-done = (f32[768,3,192]{0,2,1:T(8,128)}, f32[192,768]{1,0:T(8,128)}, f32[768,768]{1,0:T(8,128)}, f32[768,768]{1,0:T(8,128)}) async-done(((f32[768,3,192]{0,2,1:T(8,128)}, f32[192,768]{1,0:T(8,128)}, f32[768,768]{1,0:T(8,128)}, f32[768,768]{1,0:T(8,128)}), (f32[768,3,192]{0,2,1:T(8,128)}, f32[192,768]{1,0:T(8,128)}, f32[768,768]{1,0:T(8,128)}, ...) | async-done | bytes 7077904 | tf_op jit(solution)/shard_map/psum | solution.py:287
  737.7 2.9 copy.124
  (234 shorter events, 66.4 us)
Async XLA Ops:
  7.2 244.1 %copy-start = (bf16[768,768]{1,0:T(8,128)(2,1)S(1)}, bf16[768,768]{1,0:T(8,128)(2,1)}, u32[]{:S(2)}) copy-start(bf16[768,768]{1,0:T(8,128)(2,1)} %param.33) | copy-start | bytes 3538948
  7.2 14.8 %copy-start.9 = (bf16[768,3,192]{0,2,1:T(8,128)(2,1)S(1)}, bf16[768,3,192]{0,2,1:T(8,128)(2,1)}, u32[]{:S(2)}) copy-start(bf16[768,3,192]{0,2,1:T(8,128)(2,1)} %param.29) | copy-start | bytes 2654212
  7.2 64.2 %all-gather.6.cloned.1.call-start = ((), (), s32[]{:S(2)}) async-start(), calls=%async_computation.6 | async-start | bytes 1769472 | tf_op jit(solution)/shard_map/all_gather | solution.py:200
  10.0 12.6 %copy-start.36 = (f32[128]{0:T(128)}, f32[128]{0:T(128)S(1)}, u32[]{:S(2)}) copy-start(f32[128]{0:T(128)S(1)} %add_rsqrt_fusion) | copy-start | bytes 1540
  23.8 3.0 copy-start.15
  25.3 3.1 copy-start.29
  25.3 3.1 copy-start.24
  26.0 11.9 %copy-start.18 = (bf16[192,768]{1,0:T(8,128)(2,1)S(1)}, bf16[192,768]{1,0:T(8,128)(2,1)}, u32[]{:S(2)}) copy-start(bf16[192,768]{1,0:T(8,128)(2,1)} %param.31) | copy-start | bytes 884740
  26.0 90.6 %all-gather.8.cloned.1.call-start = ((), (), s32[]{:S(2)}) async-start(), calls=%async_computation.7 | async-start | bytes 1769472 | tf_op jit(solution)/shard_map/all_gather | solution.py:201
  26.8 153.4 %all-gather.4.cloned.1.call-start = ((), (), s32[]{:S(2)}) async-start(), calls=%async_computation.4 | async-start | bytes 3538944 | tf_op jit(solution)/shard_map/all_gather | solution.py:132
  27.6 380.5 %reduce-scatter.7.cloned.1.call-start = ((), (), s32[]{:S(2)}) async-start(), calls=%async_computation.8 | async-start | bytes 7077888 | tf_op jit(solution)/shard_map/reduce_scatter | solution.py:252
  217.8 2.7 copy-start.46
  241.7 9.5 %copy-start.44 = (f32[768]{0:T(1024)S(1)}, f32[768]{0:T(1024)}, u32[]{:S(2)}) copy-start(f32[768]{0:T(1024)} %param.34) | copy-start | bytes 9220
  241.7 211.1 %reduce-scatter.11.cloned.1.call-start = ((), (), s32[]{:S(2)}) async-start(), calls=%async_computation.10 | async-start | bytes 1966080 | tf_op jit(solution)/shard_map/reduce_scatter | solution.py:273
  251.2 4.5 copy-start.5
  251.2 4.5 copy-start.2
  251.3 4.5 copy-start.16
  259.8 208.4 %reduce-scatter.9.cloned.1.call-start = ((), (), s32[]{:S(2)}) async-start(), calls=%async_computation.9 | async-start | bytes 1966080 | tf_op jit(solution)/shard_map/reduce_scatter | solution.py:272
  260.6 151.7 %copy-start.20 = (f32[512,3,16]{0,2,1:T(8,128)}, f32[512,3,16]{0,2,1:T(8,128)S(1)}, u32[]{:S(2)}) copy-start(f32[512,3,16]{0,2,1:T(8,128)S(1)} %fusion.102) | copy-start | bytes 294916
  413.6 2.8 copy-start.10
  418.4 80.4 %reduce-scatter.5.cloned.1.call-start = ((), (), s32[]{:S(2)}) async-start(), calls=%async_computation.5 | async-start | bytes 1966080 | tf_op jit(solution)/shard_map/reduce_scatter | solution.py:168
  421.7 315.3 %all-reduce.5.cloned.1.call-start = ((), (), s32[]{:S(2)}) async-start(), calls=%async_computation.11 | async-start | bytes 14155776 | tf_op jit(solution)/shard_map/psum | solution.py:287
  430.9 37.4 %copy-start.8 = (bf16[128,768]{1,0:T(8,128)(2,1)S(1)}, bf16[128,768]{1,0:T(8,128)(2,1)}, u32[]{:S(2)}) copy-start(bf16[128,768]{1,0:T(8,128)(2,1)} %param.23) | copy-start | bytes 589828
  430.9 37.4 %copy-start.32 = (f32[768]{0:T(1024)S(1)}, f32[768]{0:T(1024)}, u32[]{:S(2)}) copy-start(f32[768]{0:T(1024)} %param.27) | copy-start | bytes 9220
  430.9 37.4 %copy-start.33 = (f32[768]{0:T(1024)S(1)}, f32[768]{0:T(1024)}, u32[]{:S(2)}) copy-start(f32[768]{0:T(1024)} %param.25) | copy-start | bytes 9220
  430.9 37.3 %copy-start.37 = (f32[128]{0:T(128)S(1)}, f32[128]{0:T(128)}, u32[]{:S(2)}) copy-start(f32[128]{0:T(128)} %copy-done.36) | copy-start | bytes 1540
  430.9 67.9 %copy-start.38 = (f32[768]{0:T(1024)S(1)}, f32[768]{0:T(1024)}, u32[]{:S(2)}) copy-start(f32[768]{0:T(1024)} %param.36) | copy-start | bytes 9220
  430.9 67.9 %copy-start.39 = (f32[768]{0:T(1024)S(1)}, f32[768]{0:T(1024)}, u32[]{:S(2)}) copy-start(f32[768]{0:T(1024)} %param.32) | copy-start | bytes 9220
  431.9 66.9 %copy-start.25 = (bf16[128,768]{1,0:T(8,128)(2,1)S(1)}, bf16[128,768]{1,0:T(8,128)(2,1)}, u32[]{:S(2)}) copy-start(bf16[128,768]{1,0:T(8,128)(2,1)} %param.37) | copy-start | bytes 589828
  544.1 196.5 %copy-start.40 = (f32[768]{0:T(1024)}, f32[768]{0:T(1024)S(1)}, u32[]{:S(2)}) copy-start(f32[768]{0:T(1024)S(1)} %get-tuple-element.1289) | copy-start | bytes 9220
  737.7 3.0 copy-start.28
  737.7 3.8 copy-start.14
  (29 other events, 49.5 us)
Sparse Core Ops, SparseCore 0:
  26.1 45.2 all-gather.5
  74.0 42.5 all-gather.7
  119.3 60.8 all-gather.3
  241.8 166.2 reduce-scatter.6
  410.5 27.2 reduce-scatter.10
  440.2 27.9 reduce-scatter.8
  470.8 27.9 reduce-scatter.4
  504.4 232.6 all-reduce.4
